TPU v7x, 128 devices: a whole 4x4x4 slice. The times are simulated.
128 devices in a mesh: dp: 8 (over x, core), seq: 16 (over y, z).
Axes of the slice: x: 4, y: 4, z: 4, core: 2. Of those that a mesh axis runs over, the one named last changes fastest.
Arguments:
- queries: bfloat16 [16, 98304, 128], P(None, ('dp', 'seq')), parts along dimension 1, may hold values from -6 to 6
- key_rows: bfloat16 [16, 98304, 128], P(None, ('dp', 'seq')), parts along dimension 1, may hold values from -6 to 6
- value_rows: bfloat16 [16, 98304, 128], P(None, ('dp', 'seq')), parts along dimension 1, may hold values from -6 to 6
- out_grad: bfloat16 [16, 98304, 128], P(None, ('dp', 'seq')), parts along dimension 1, may hold values from -6 to 6
Outputs:
- attended: bfloat16 [16, 98304, 128], P(None, ('dp', 'seq')), parts along dimension 1
- grad_queries: bfloat16 [16, 98304, 128], P(None, ('dp', 'seq')), parts along dimension 1
- grad_keys: bfloat16 [16, 98304, 128], P(None, ('dp', 'seq')), parts along dimension 1
- grad_values: bfloat16 [16, 98304, 128], P(None, ('dp', 'seq')), parts along dimension 1
There are 8 independent parts, one for each index of `dp`. A program takes and returns all parts, laid end to end along the dimension named above; each array names one. Nothing has to cross between parts.
All inputs are finite; a program needn't handle non-finite values.
Results may differ from a plain program's by a relative error of at most 0.009.
Values may be sent and summed in bfloat16 or wider, within the bound.
A program may use at most 192 MiB of HBM per device.

v0:
```python
import jax
import jax.numpy as jnp
from jax import lax
from jax.sharding import PartitionSpec as P


def group_terms(pieces):
    q_blk, k_blk, v_blk, g_blk, pre_blk, suf_blk = pieces
    wide = jnp.float32
    length = q_blk.shape[1]
    rows_idx = jnp.arange(length, dtype=jnp.int32)
    causal = rows_idx[:, None] >= rows_idx[None, :]
    scores = jnp.einsum("htd,hsd->hts", q_blk, k_blk, preferred_element_type=wide)
    masked = jnp.where(causal[None], scores, 0.0).astype(jnp.bfloat16)
    dots = jnp.einsum("htd,hsd->hts", g_blk, v_blk, preferred_element_type=wide)
    mdots = jnp.where(causal[None], dots, 0.0).astype(jnp.bfloat16)
    inner = jnp.einsum("hts,hsd->htd", masked, v_blk, preferred_element_type=wide) + jnp.einsum(
        "hta,hab->htb", q_blk, pre_blk, preferred_element_type=wide
    )
    dq_full = jnp.einsum("hts,hsd->htd", mdots, k_blk, preferred_element_type=wide) + jnp.einsum(
        "htb,hab->hta", g_blk, pre_blk, preferred_element_type=wide
    )
    dk_full = jnp.einsum("hts,htd->hsd", mdots, q_blk, preferred_element_type=wide) + jnp.einsum(
        "hsb,hab->hsa", v_blk, suf_blk, preferred_element_type=wide
    )
    dv_full = jnp.einsum("hts,htd->hsd", masked, g_blk, preferred_element_type=wide) + jnp.einsum(
        "hsa,hab->hsb", k_blk, suf_blk, preferred_element_type=wide
    )
    return (
        inner,
        dq_full.astype(jnp.bfloat16),
        dk_full.astype(jnp.bfloat16),
        dv_full.astype(jnp.bfloat16),
    )


def on_device(queries, key_rows, value_rows, out_grad):
    wide = jnp.float32
    heads, length, width = queries.shape
    my_index = lax.axis_index("seq")
    count = lax.axis_size("seq")
    position = (my_index * length + jnp.arange(length, dtype=jnp.int32)).astype(wide)
    scale = 1.0 / jnp.sqrt(width * (position + 1.0))
    scaled_grad = (scale[None, :, None] * out_grad.astype(wide)).astype(jnp.bfloat16)
    key_state = jnp.einsum(
        "hta,htb->hab", key_rows, value_rows, preferred_element_type=wide
    ).astype(jnp.bfloat16)
    grad_state = jnp.einsum(
        "hta,htb->hab", queries, scaled_grad, preferred_element_type=wide
    ).astype(jnp.bfloat16)
    ranks = jnp.arange(count, dtype=jnp.int32)
    earlier = (ranks < my_index).astype(jnp.bfloat16)
    later = (ranks > my_index).astype(jnp.bfloat16)
    all_keys = lax.all_gather(key_state[None], "seq", axis=0, tiled=True)
    prefix = jnp.einsum("n,nhab->hab", earlier, all_keys, preferred_element_type=wide)
    all_grads = lax.all_gather(grad_state[None], "seq", axis=0, tiled=True)
    suffix = jnp.einsum("n,nhab->hab", later, all_grads, preferred_element_type=wide)
    prefix_half = prefix.astype(jnp.bfloat16)
    suffix_half = suffix.astype(jnp.bfloat16)
    group = 4
    steps_count = heads // group

    def grouped(array):
        return array.reshape((steps_count, group) + array.shape[1:])

    inner, grad_q, grad_k, grad_v = lax.map(
        group_terms,
        (
            grouped(queries),
            grouped(key_rows),
            grouped(value_rows),
            grouped(scaled_grad),
            grouped(prefix_half),
            grouped(suffix_half),
        ),
    )
    attended = (scale[None, :, None] * inner.reshape(heads, length, width)).astype(jnp.bfloat16)
    return (
        attended,
        grad_q.reshape(heads, length, width),
        grad_k.reshape(heads, length, width),
        grad_v.reshape(heads, length, width),
    )


def solution(mesh):
    placed = (
        P(None, ("dp", "seq"), None),
        P(None, ("dp", "seq"), None),
        P(None, ("dp", "seq"), None),
        P(None, ("dp", "seq"), None),
    )
    return jax.shard_map(
        on_device,
        mesh=mesh,
        in_specs=placed,
        out_specs=(
            P(None, ("dp", "seq"), None),
            P(None, ("dp", "seq"), None),
            P(None, ("dp", "seq"), None),
            P(None, ("dp", "seq"), None),
        ),
        check_vma=False,
    )
```

profile of v0, /device:TPU:0, one launch (start us, length us, event | category | flops | bytes accessed | tf_op | source)
XLA Modules:
  0.0 249.2 jit_solution(6098355292058006964)
XLA Ops:
  7.2 4.7 %convolution_convert_fusion.1 = bf16[16,128,128]{2,1,0:T(8,128)(2,1)} fusion(bf16[16,768,128]{2,1,0:T(8,128)(2,1)} %param.7, bf16[16,768,128]{2,1,0:T(8,128)(2,1)} %param.8), kind=kOutput, calls=%fused_computation.67 | convolution fusion | flops 402915328 | bytes 6815744 | tf_op jit(solution)/shard_map/hta,htb->hab/dot_general | solution.py:45
  12.0 2.9 %multiply_convert_fusion = bf16[16,768,128]{2,1,0:T(8,128)(2,1)S(1)} fusion(bf16[16,768,128]{2,1,0:T(8,128)(2,1)} %param.9, f32[768]{0:T(1024)S(1)} %multiply_rsqrt_fusion), kind=kLoop, calls=%fused_computation.65 | loop fusion | flops 4718592 | bytes 6294528 | tf_op jit(solution)/shard_map/convert_element_type | solution.py:44
  19.0 66.5 %all-gather.5.cloned.1.call-done = bf16[256,128,128]{2,1,0:T(8,128)(2,1)} async-done(((bf16[16,128,128]{2,1,0:T(8,128)(2,1)}), bf16[256,128,128]{2,1,0:T(8,128)(2,1)}) %all-gather.5.cloned.1.call-update) | async-done | bytes 8388624 | tf_op jit(solution)/shard_map/all_gather | solution.py:54
  85.5 8.3 %fusion.54 = f32[1,16,128,128]{3,0,2,1:T(1,128)S(1)} fusion(bf16[16,16,128,128]{3,2,1,0:T(8,128)(2,1)} %bitcast.143, s32[]{:T(128)S(6)} %axis_index.12), kind=kOutput, calls=%fused_computation.61 | convolution fusion | flops 8388624 | bytes 9437188 | tf_op jit(solution)/shard_map/n,nhab->hab/dot_general | solution.py:55
  94.7 63.5 %all-gather.7.cloned.1.call-done = bf16[256,128,128]{2,1,0:T(8,128)(2,1)} async-done(((bf16[16,128,128]{2,1,0:T(8,128)(2,1)}), bf16[256,128,128]{2,1,0:T(8,128)(2,1)}) %all-gather.7.cloned.1.call-update) | async-done | bytes 8388624 | tf_op jit(solution)/shard_map/all_gather | solution.py:56
  158.2 8.5 %fusion.52 = f32[1,16,128,128]{3,0,2,1:T(1,128)S(1)} fusion(bf16[16,16,128,128]{3,2,1,0:T(8,128)(2,1)} %bitcast.144, s32[]{:T(128)S(6)} %axis_index.12), kind=kOutput, calls=%fused_computation.59 | convolution fusion | flops 8388624 | bytes 9437188 | tf_op jit(solution)/shard_map/n,nhab->hab/dot_general | solution.py:57
  167.6 69.6 %while.16 = (s32[]{:T(128)}, f32[4,4,768,128]{3,2,1,0:T(8,128)}, bf16[4,4,768,128]{3,2,1,0:T(8,128)(2,1)}, bf16[4,4,768,128]{3,2,1,0:T(8,128)(2,1)}, bf16[4,4,76...) while((s32[]{:T(128)}, f32[4,4,768,128]{3,2,1,0:T(8,128)}, ...), condition=%wide.region_1.2_spmd, body=%wide.region_0.1_spmd.sunk | while | flops 4039311360 | bytes 96413928 | solution.py:66
  173.4 2.6 %fusion.125 = bf16[4,4,768,128]{3,2,1,0:T(8,128)(2,1)} fusion(bf16[4,4,768,128]{3,2,1,0:T(8,128)(2,1)} %get-tuple-element.172, s32[]{:T(128)S(6)} %copy.40, f32[4,768,128]{2,1,0:T(8,128)S(1)} %fusion.124, bf16[4,768,768]{2,1,0:T(8,128)(2,1)S(1)} %select_convert_fusion.5, bf16[4,4,768,128]{3,2,1,0:T(8,128)(2,1)S(1)} %copy-done.1), kind=kOutput, calls=%fused_computation.10.clone.1 | convolution fusion | flops 604766208 | bytes 7865344 | tf_op jit(solution)/shard_map/while/body/eval_jaxpr/hts,htd->hsd/dot_general | solution.py:23
  176.0 2.3 fusion.123
  179.8 2.6 %fusion.127 = bf16[4,4,768,128]{3,2,1,0:T(8,128)(2,1)} fusion(bf16[4,4,768,128]{3,2,1,0:T(8,128)(2,1)} %get-tuple-element.173, s32[]{:T(128)S(6)} %copy.40, f32[4,768,128]{2,1,0:T(8,128)S(1)} %fusion.126, bf16[4,768,768]{2,1,0:T(8,128)(2,1)S(1)} %select_convert_fusion.4, bf16[4,4,768,128]{3,2,1,0:T(8,128)(2,1)S(1)} %get-tuple-element.190), kind=kOutput, calls=%fused_computation.12.clone.1 | convolution fusion | flops 604766208 | bytes 7865344 | tf_op jit(solution)/shard_map/while/body/eval_jaxpr/hts,htd->hsd/dot_general | solution.py:26
  182.4 2.6 %bitcast_dynamic-update-slice_fusion.2 = f32[4,4,768,128]{3,2,1,0:T(8,128)} fusion(f32[4,4,768,128]{3,2,1,0:T(8,128)} %get-tuple-element.170, s32[]{:T(128)S(6)} %copy.40, f32[4,768,128]{2,1,0:T(8,128)S(1)} %fusion.121, bf16[4,768,768]{2,1,0:T(8,128)(2,1)S(1)} %select_convert_fusion.4, bf16[4,4,768,128]{3,2,1,0:T(8,128)(2,1)S(1)} %copy-done.2), kind=kOutput, calls=%fused_computation.3.clone.1 | convolution fusion | flops 604372992 | bytes 8651776 | tf_op jit(solution)/shard_map/while/body/eval_jaxpr/hts,hsd->htd/dot_general | solution.py:17
  190.8 2.6 %fusion.125 = bf16[4,4,768,128]{3,2,1,0:T(8,128)(2,1)} fusion(bf16[4,4,768,128]{3,2,1,0:T(8,128)(2,1)} %get-tuple-element.172, s32[]{:T(128)S(6)} %copy.40, f32[4,768,128]{2,1,0:T(8,128)S(1)} %fusion.124, bf16[4,768,768]{2,1,0:T(8,128)(2,1)S(1)} %select_convert_fusion.5, bf16[4,4,768,128]{3,2,1,0:T(8,128)(2,1)S(1)} %copy-done.1), kind=kOutput, calls=%fused_computation.10.clone.1 | convolution fusion | flops 604766208 | bytes 7865344 | tf_op jit(solution)/shard_map/while/body/eval_jaxpr/hts,htd->hsd/dot_general | solution.py:23
  193.4 2.3 fusion.123
  197.2 2.6 %fusion.127 = bf16[4,4,768,128]{3,2,1,0:T(8,128)(2,1)} fusion(bf16[4,4,768,128]{3,2,1,0:T(8,128)(2,1)} %get-tuple-element.173, s32[]{:T(128)S(6)} %copy.40, f32[4,768,128]{2,1,0:T(8,128)S(1)} %fusion.126, bf16[4,768,768]{2,1,0:T(8,128)(2,1)S(1)} %select_convert_fusion.4, bf16[4,4,768,128]{3,2,1,0:T(8,128)(2,1)S(1)} %get-tuple-element.190), kind=kOutput, calls=%fused_computation.12.clone.1 | convolution fusion | flops 604766208 | bytes 7865344 | tf_op jit(solution)/shard_map/while/body/eval_jaxpr/hts,htd->hsd/dot_general | solution.py:26
  199.8 2.6 %bitcast_dynamic-update-slice_fusion.2 = f32[4,4,768,128]{3,2,1,0:T(8,128)} fusion(f32[4,4,768,128]{3,2,1,0:T(8,128)} %get-tuple-element.170, s32[]{:T(128)S(6)} %copy.40, f32[4,768,128]{2,1,0:T(8,128)S(1)} %fusion.121, bf16[4,768,768]{2,1,0:T(8,128)(2,1)S(1)} %select_convert_fusion.4, bf16[4,4,768,128]{3,2,1,0:T(8,128)(2,1)S(1)} %copy-done.2), kind=kOutput, calls=%fused_computation.3.clone.1 | convolution fusion | flops 604372992 | bytes 8651776 | tf_op jit(solution)/shard_map/while/body/eval_jaxpr/hts,hsd->htd/dot_general | solution.py:17
  208.1 2.6 %fusion.125 = bf16[4,4,768,128]{3,2,1,0:T(8,128)(2,1)} fusion(bf16[4,4,768,128]{3,2,1,0:T(8,128)(2,1)} %get-tuple-element.172, s32[]{:T(128)S(6)} %copy.40, f32[4,768,128]{2,1,0:T(8,128)S(1)} %fusion.124, bf16[4,768,768]{2,1,0:T(8,128)(2,1)S(1)} %select_convert_fusion.5, bf16[4,4,768,128]{3,2,1,0:T(8,128)(2,1)S(1)} %copy-done.1), kind=kOutput, calls=%fused_computation.10.clone.1 | convolution fusion | flops 604766208 | bytes 7865344 | tf_op jit(solution)/shard_map/while/body/eval_jaxpr/hts,htd->hsd/dot_general | solution.py:23
  210.8 2.3 fusion.123
  214.5 2.6 %fusion.127 = bf16[4,4,768,128]{3,2,1,0:T(8,128)(2,1)} fusion(bf16[4,4,768,128]{3,2,1,0:T(8,128)(2,1)} %get-tuple-element.173, s32[]{:T(128)S(6)} %copy.40, f32[4,768,128]{2,1,0:T(8,128)S(1)} %fusion.126, bf16[4,768,768]{2,1,0:T(8,128)(2,1)S(1)} %select_convert_fusion.4, bf16[4,4,768,128]{3,2,1,0:T(8,128)(2,1)S(1)} %get-tuple-element.190), kind=kOutput, calls=%fused_computation.12.clone.1 | convolution fusion | flops 604766208 | bytes 7865344 | tf_op jit(solution)/shard_map/while/body/eval_jaxpr/hts,htd->hsd/dot_general | solution.py:26
  217.2 2.6 %bitcast_dynamic-update-slice_fusion.2 = f32[4,4,768,128]{3,2,1,0:T(8,128)} fusion(f32[4,4,768,128]{3,2,1,0:T(8,128)} %get-tuple-element.170, s32[]{:T(128)S(6)} %copy.40, f32[4,768,128]{2,1,0:T(8,128)S(1)} %fusion.121, bf16[4,768,768]{2,1,0:T(8,128)(2,1)S(1)} %select_convert_fusion.4, bf16[4,4,768,128]{3,2,1,0:T(8,128)(2,1)S(1)} %copy-done.2), kind=kOutput, calls=%fused_computation.3.clone.1 | convolution fusion | flops 604372992 | bytes 8651776 | tf_op jit(solution)/shard_map/while/body/eval_jaxpr/hts,hsd->htd/dot_general | solution.py:17
  225.5 2.6 %fusion.125 = bf16[4,4,768,128]{3,2,1,0:T(8,128)(2,1)} fusion(bf16[4,4,768,128]{3,2,1,0:T(8,128)(2,1)} %get-tuple-element.172, s32[]{:T(128)S(6)} %copy.40, f32[4,768,128]{2,1,0:T(8,128)S(1)} %fusion.124, bf16[4,768,768]{2,1,0:T(8,128)(2,1)S(1)} %select_convert_fusion.5, bf16[4,4,768,128]{3,2,1,0:T(8,128)(2,1)S(1)} %copy-done.1), kind=kOutput, calls=%fused_computation.10.clone.1 | convolution fusion | flops 604766208 | bytes 7865344 | tf_op jit(solution)/shard_map/while/body/eval_jaxpr/hts,htd->hsd/dot_general | solution.py:23
  228.1 2.3 fusion.123
  231.9 2.6 %fusion.127 = bf16[4,4,768,128]{3,2,1,0:T(8,128)(2,1)} fusion(bf16[4,4,768,128]{3,2,1,0:T(8,128)(2,1)} %get-tuple-element.173, s32[]{:T(128)S(6)} %copy.40, f32[4,768,128]{2,1,0:T(8,128)S(1)} %fusion.126, bf16[4,768,768]{2,1,0:T(8,128)(2,1)S(1)} %select_convert_fusion.4, bf16[4,4,768,128]{3,2,1,0:T(8,128)(2,1)S(1)} %get-tuple-element.190), kind=kOutput, calls=%fused_computation.12.clone.1 | convolution fusion | flops 604766208 | bytes 7865344 | tf_op jit(solution)/shard_map/while/body/eval_jaxpr/hts,htd->hsd/dot_general | solution.py:26
  234.5 2.6 %bitcast_dynamic-update-slice_fusion.2 = f32[4,4,768,128]{3,2,1,0:T(8,128)} fusion(f32[4,4,768,128]{3,2,1,0:T(8,128)} %get-tuple-element.170, s32[]{:T(128)S(6)} %copy.40, f32[4,768,128]{2,1,0:T(8,128)S(1)} %fusion.121, bf16[4,768,768]{2,1,0:T(8,128)(2,1)S(1)} %select_convert_fusion.4, bf16[4,4,768,128]{3,2,1,0:T(8,128)(2,1)S(1)} %copy-done.2), kind=kOutput, calls=%fused_computation.3.clone.1 | convolution fusion | flops 604372992 | bytes 8651776 | tf_op jit(solution)/shard_map/while/body/eval_jaxpr/hts,hsd->htd/dot_general | solution.py:17
  237.1 5.2 %fusion.56 = bf16[16,768,128]{2,1,0:T(8,128)(2,1)} fusion(f32[4,4,768,128]{3,2,1,0:T(8,128)} %get-tuple-element.64, f32[768]{0:T(1024)S(1)} %multiply_rsqrt_fusion), kind=kLoop, calls=%fused_computation.64 | loop fusion | flops 3145728 | bytes 9440256 | tf_op jit(solution)/shard_map/convert_element_type | solution.py:77
  (75 shorter events, 34.7 us)
Async XLA Ops:
  7.2 78.4 %all-gather.5.cloned.1.call-start = ((), (), s32[]{:S(2)}) async-start(), calls=%async_computation | async-start | bytes 8912896 | tf_op jit(solution)/shard_map/all_gather | solution.py:54
  11.9 146.3 %all-gather.7.cloned.1.call-start = ((), (), s32[]{:S(2)}) async-start(), calls=%async_computation.1 | async-start | bytes 8912896 | tf_op jit(solution)/shard_map/all_gather | solution.py:56
  12.0 3.0 %copy-start = (bf16[16,768,128]{2,1,0:T(8,128)(2,1)S(1)}, bf16[16,768,128]{2,1,0:T(8,128)(2,1)}, u32[]{:S(2)}) copy-start(bf16[16,768,128]{2,1,0:T(8,128)(2,1)} %param.6) | copy-start | bytes 9437188
  167.6 3.5 %copy-start.1 = (bf16[4,4,768,128]{3,2,1,0:T(8,128)(2,1)S(1)}, bf16[4,4,768,128]{3,2,1,0:T(8,128)(2,1)}, u32[]{:S(2)}) copy-start(bf16[4,4,768,128]{3,2,1,0:T(8,128)(2,1)} %get-tuple-element.186) | copy-start | bytes 9437188 | tf_op jit(solution)/shard_map/while
  167.6 3.5 %copy-start.4 = (bf16[4,4,128,128]{3,2,1,0:T(8,128)(2,1)S(1)}, bf16[4,4,128,128]{3,2,1,0:T(8,128)(2,1)}, u32[]{:S(2)}) copy-start(bf16[4,4,128,128]{3,2,1,0:T(8,128)(2,1)} %get-tuple-element.189) | copy-start | bytes 1572868 | tf_op jit(solution)/shard_map/while
  169.4 2.4 copy-start.2
  173.3 2.6 %copy-start.3 = (bf16[4,4,768,128]{3,2,1,0:T(8,128)(2,1)S(1)}, bf16[4,4,768,128]{3,2,1,0:T(8,128)(2,1)}, u32[]{:S(2)}) copy-start(bf16[4,4,768,128]{3,2,1,0:T(8,128)(2,1)} %get-tuple-element.187) | copy-start | bytes 9437188 | tf_op jit(solution)/shard_map/while
  185.0 3.5 %copy-start.1 = (bf16[4,4,768,128]{3,2,1,0:T(8,128)(2,1)S(1)}, bf16[4,4,768,128]{3,2,1,0:T(8,128)(2,1)}, u32[]{:S(2)}) copy-start(bf16[4,4,768,128]{3,2,1,0:T(8,128)(2,1)} %get-tuple-element.186) | copy-start | bytes 9437188 | tf_op jit(solution)/shard_map/while
  185.0 3.5 %copy-start.4 = (bf16[4,4,128,128]{3,2,1,0:T(8,128)(2,1)S(1)}, bf16[4,4,128,128]{3,2,1,0:T(8,128)(2,1)}, u32[]{:S(2)}) copy-start(bf16[4,4,128,128]{3,2,1,0:T(8,128)(2,1)} %get-tuple-element.189) | copy-start | bytes 1572868 | tf_op jit(solution)/shard_map/while
  186.8 2.4 copy-start.2
  190.7 2.6 %copy-start.3 = (bf16[4,4,768,128]{3,2,1,0:T(8,128)(2,1)S(1)}, bf16[4,4,768,128]{3,2,1,0:T(8,128)(2,1)}, u32[]{:S(2)}) copy-start(bf16[4,4,768,128]{3,2,1,0:T(8,128)(2,1)} %get-tuple-element.187) | copy-start | bytes 9437188 | tf_op jit(solution)/shard_map/while
  202.3 3.5 %copy-start.1 = (bf16[4,4,768,128]{3,2,1,0:T(8,128)(2,1)S(1)}, bf16[4,4,768,128]{3,2,1,0:T(8,128)(2,1)}, u32[]{:S(2)}) copy-start(bf16[4,4,768,128]{3,2,1,0:T(8,128)(2,1)} %get-tuple-element.186) | copy-start | bytes 9437188 | tf_op jit(solution)/shard_map/while
  202.3 3.5 %copy-start.4 = (bf16[4,4,128,128]{3,2,1,0:T(8,128)(2,1)S(1)}, bf16[4,4,128,128]{3,2,1,0:T(8,128)(2,1)}, u32[]{:S(2)}) copy-start(bf16[4,4,128,128]{3,2,1,0:T(8,128)(2,1)} %get-tuple-element.189) | copy-start | bytes 1572868 | tf_op jit(solution)/shard_map/while
  204.2 2.4 copy-start.2
  208.1 2.6 %copy-start.3 = (bf16[4,4,768,128]{3,2,1,0:T(8,128)(2,1)S(1)}, bf16[4,4,768,128]{3,2,1,0:T(8,128)(2,1)}, u32[]{:S(2)}) copy-start(bf16[4,4,768,128]{3,2,1,0:T(8,128)(2,1)} %get-tuple-element.187) | copy-start | bytes 9437188 | tf_op jit(solution)/shard_map/while
  219.7 3.5 %copy-start.1 = (bf16[4,4,768,128]{3,2,1,0:T(8,128)(2,1)S(1)}, bf16[4,4,768,128]{3,2,1,0:T(8,128)(2,1)}, u32[]{:S(2)}) copy-start(bf16[4,4,768,128]{3,2,1,0:T(8,128)(2,1)} %get-tuple-element.186) | copy-start | bytes 9437188 | tf_op jit(solution)/shard_map/while
  219.7 3.5 %copy-start.4 = (bf16[4,4,128,128]{3,2,1,0:T(8,128)(2,1)S(1)}, bf16[4,4,128,128]{3,2,1,0:T(8,128)(2,1)}, u32[]{:S(2)}) copy-start(bf16[4,4,128,128]{3,2,1,0:T(8,128)(2,1)} %get-tuple-element.189) | copy-start | bytes 1572868 | tf_op jit(solution)/shard_map/while
  221.6 2.4 copy-start.2
  225.5 2.6 %copy-start.3 = (bf16[4,4,768,128]{3,2,1,0:T(8,128)(2,1)S(1)}, bf16[4,4,768,128]{3,2,1,0:T(8,128)(2,1)}, u32[]{:S(2)}) copy-start(bf16[4,4,768,128]{3,2,1,0:T(8,128)(2,1)} %get-tuple-element.187) | copy-start | bytes 9437188 | tf_op jit(solution)/shard_map/while
Sparse Core Ops, SparseCore 0:
  12.1 73.4 all-gather.4
  87.7 70.4 all-gather.6
where the time goes:
time: 250 us; the launch traced here: 249 us
  waiting for transfers between devices  130 us (52%)
  matrix products  91.8 us (37%)
  between operations  14.1 us (6%)
  other arithmetic  10.7 us (4%)
    all_gather x1, waiting for transfers between devices, on_device(): all_keys = lax.all_gather(key_state[None], 'seq', axis=0, tiled=True)  66.5 us
    all_gather x1, waiting for transfers between devices, on_device(): all_grads = lax.all_gather(grad_state[None], 'seq', axis=0, tiled=True)  63.5 us
    dot_general x4, matrix products, group_terms(): jnp.einsum('hts,htd->hsd', masked, g_blk, preferred_element_type=wide)  10.5 us
    dot_general x4, matrix products, group_terms(): jnp.einsum('hts,htd->hsd', mdots, q_blk, preferred_element_type=wide)  10.4 us
    dot_general x4, matrix products, group_terms(): jnp.einsum('hts,hsd->htd', masked, v_blk, preferred_element_type=wide)  10.3 us
    dot_general x4, matrix products, group_terms(): jnp.einsum('hts,hsd->htd', mdots, k_blk, preferred_element_type=wide)  9.14 us
    dot_general x1, matrix products, on_device(): jnp.einsum('n,nhab->hab', later, all_grads, preferred_element_type=wide)  8.47 us
    dot_general x1, matrix products, on_device(): jnp.einsum('n,nhab->hab', earlier, all_keys, preferred_element_type=wide)  8.3 us
  transfers between devices with their start and end apart: 2, of which 2 were waited for; matrix products, arithmetic and copies ran while one was open for 6% of the time, Pallas kernels for 0%

commit v1 on v0

v1 whole, which is shorter than its diff:
```python
import functools

import jax
import jax.numpy as jnp
from jax import lax
from jax.experimental import pallas as pl
from jax.experimental.pallas import tpu as pltpu
from jax.sharding import PartitionSpec as P

MESH = pl.DeviceIdType.MESH
WIDE = jnp.float32
HALF = jnp.bfloat16
CHUNK = 256
EARLY = 8


def nn(a, b):
    return lax.dot_general(a, b, (((1,), (0,)), ((), ())), preferred_element_type=WIDE)


def nt(a, b):
    return lax.dot_general(a, b, (((1,), (1,)), ((), ())), preferred_element_type=WIDE)


def tn(a, b):
    return lax.dot_general(a, b, (((0,), (0,)), ((), ())), preferred_element_type=WIDE)


def states_kernel(
    side, q_in, k_in, v_in, g_in,
    q_ref, k_ref, v_ref, g_ref, att_ref, dq_ref, dk_ref, dv_ref, pre_ref, suf_ref, got_ref, scale_ref,
    send1, recv1, send2, in_sem, ss1, rs1, ss2, rs2,
):
    heads, length, width = q_in.shape
    chunks = length // CHUNK
    me = lax.axis_index("seq")
    count = heads

    def loads(h):
        pairs = ((k_in, k_ref), (v_in, v_ref), (q_in, q_ref), (g_in, g_ref))
        return [
            pltpu.make_async_copy(src.at[h], dst.at[h], in_sem.at[h, i])
            for i, (src, dst) in enumerate(pairs)
        ]

    def peer(i):
        row, col = me // side, me % side
        return ((row + i // side) % side) * side + (col + i % side) % side

    @pl.loop(0, count)
    def _(i):
        for copy in loads(peer((i + 1) % count)):
            copy.start()

    barrier = pltpu.get_barrier_semaphore()

    @pl.loop(1, count)
    def _(i):
        pl.semaphore_signal(barrier, inc=1, device_id={"seq": peer(i)}, device_id_type=MESH)

    position = (me * length + lax.broadcasted_iota(jnp.int32, (length, width), 0)).astype(WIDE)
    scale_ref[...] = 1.0 / jnp.sqrt(width * (position + 1.0))
    pl.semaphore_wait(barrier, count - 1)

    def first(h):
        return pltpu.make_async_remote_copy(
            src_ref=send1.at[h], dst_ref=recv1.at[me], send_sem=ss1.at[h], recv_sem=rs1.at[me],
            device_id={"seq": h}, device_id_type=MESH,
        )

    def second(j):
        return pltpu.make_async_remote_copy(
            src_ref=send2.at[j], dst_ref=got_ref.at[me], send_sem=ss2.at[j], recv_sem=rs2.at[me],
            device_id={"seq": j}, device_id_type=MESH,
        )

    def first_from(j):
        return pltpu.make_async_remote_copy(
            src_ref=send1.at[j], dst_ref=recv1.at[j], send_sem=ss1.at[j], recv_sem=rs1.at[j],
            device_id={"seq": j}, device_id_type=MESH,
        )

    def second_from(j):
        return pltpu.make_async_remote_copy(
            src_ref=send2.at[j], dst_ref=got_ref.at[j], send_sem=ss2.at[j], recv_sem=rs2.at[j],
            device_id={"seq": j}, device_id_type=MESH,
        )

    def form_states(h, out):
        for copy in loads(h):
            copy.wait()
        key_sum, grads = None, []
        for c in range(chunks):
            rows = pl.ds(c * CHUNK, CHUNK)
            scaled = (scale_ref[rows, :] * g_ref[h, rows, :].astype(WIDE)).astype(HALF)
            g_ref[h, rows, :] = scaled
            key = tn(k_ref[h, rows, :], v_ref[h, rows, :])
            grads.append(tn(q_ref[h, rows, :], scaled))
            if c:
                pre_ref[h, c - 1] = key_sum
            key_sum = key if c == 0 else key_sum + key
        total = None
        for c in reversed(range(chunks)):
            if c < chunks - 1:
                suf_ref[h, c] = total
            total = grads[c] if total is None else total + grads[c]
        out[0] = key_sum.astype(HALF)
        out[1] = total.astype(HALF)

    @pl.loop(1, count)
    def _(i):
        h = peer(i)
        form_states(h, send1.at[h])
        first(h).start()

    form_states(me, recv1.at[me])

    causal = lax.broadcasted_iota(jnp.int32, (CHUNK, CHUNK), 0) >= lax.broadcasted_iota(
        jnp.int32, (CHUNK, CHUNK), 1
    )

    def inside(h):
        for c in range(chunks):
            rows = pl.ds(c * CHUNK, CHUNK)
            q, k, v, g = q_ref[h, rows, :], k_ref[h, rows, :], v_ref[h, rows, :], g_ref[h, rows, :]
            scores = jnp.where(causal, nt(q, k), 0.0).astype(HALF)
            dots = jnp.where(causal, nt(g, v), 0.0).astype(HALF)
            att_ref[h, rows, :] = nn(scores, v)
            dq_ref[h, rows, :] = nn(dots, k)
            dk_ref[h, rows, :] = tn(dots, q)
            dv_ref[h, rows, :] = tn(scores, g)

    @pl.loop(0, EARLY)
    def _(h):
        inside(h)

    @pl.loop(1, count)
    def _(i):
        first_from(peer(i)).wait_recv()

    total = jnp.zeros((width, width), WIDE)
    for j in range(count):
        send2[j, 0] = total.astype(HALF)
        total = total + recv1[j, 0].astype(WIDE)
    total = jnp.zeros((width, width), WIDE)
    for j in reversed(range(count)):
        send2[j, 1] = total.astype(HALF)
        total = total + recv1[j, 1].astype(WIDE)

    @pl.loop(1, count)
    def _(i):
        second(peer(i)).start()

    got_ref[me] = send2[me]

    @pl.loop(EARLY, heads)
    def _(h):
        inside(h)

    @pl.loop(1, count)
    def _(i):
        second_from(peer(i)).wait_recv()

    @pl.loop(1, count)
    def _(i):
        first(peer(i)).wait_send()
        second(peer(i)).wait_send()


def finish_kernel(
    q_ref, k_ref, v_ref, g_ref, att_in, dq_in, dk_in, dv_in, pre_ref, suf_ref, got_ref, scale_ref,
    att_ref, dq_ref, dk_ref, dv_ref,
):
    h = pl.program_id(0)
    chunks = q_ref.shape[1] // CHUNK
    prefix, suffix = got_ref[h, 0].astype(WIDE), got_ref[h, 1].astype(WIDE)
    for c in range(chunks):
        rows = pl.ds(c * CHUNK, CHUNK)
        before = (prefix + pre_ref[h, c - 1] if c else prefix).astype(HALF)
        after = (suffix + suf_ref[h, c] if c < chunks - 1 else suffix).astype(HALF)
        q, k, v, g = q_ref[h, rows, :], k_ref[h, rows, :], v_ref[h, rows, :], g_ref[h, rows, :]
        att_ref[0, rows, :] = (scale_ref[rows, :] * (att_in[h, rows, :] + nn(q, before))).astype(HALF)
        dq_ref[0, rows, :] = (dq_in[h, rows, :] + nt(g, before)).astype(HALF)
        dk_ref[0, rows, :] = (dk_in[h, rows, :] + nt(v, after)).astype(HALF)
        dv_ref[0, rows, :] = (dv_in[h, rows, :] + nn(k, after)).astype(HALF)


def on_device(side, queries, key_rows, value_rows, out_grad):
    heads, length, width = queries.shape
    chunks = length // CHUNK
    rows = [pltpu.VMEM((heads, length, width), HALF)] * 4
    parts = [pltpu.VMEM((heads, length, width), WIDE)] * 4
    inner = [pltpu.VMEM((heads, chunks - 1, width, width), WIDE)] * 2
    got = [pltpu.VMEM((heads, 2, width, width), HALF)]
    scale = [pltpu.VMEM((length, width), WIDE)]
    vmem = pl.BlockSpec(memory_space=pltpu.VMEM)
    held = pl.pallas_call(
        functools.partial(states_kernel, side),
        out_shape=rows + parts + inner + got + scale,
        in_specs=[pl.BlockSpec(memory_space=pl.ANY)] * 4,
        out_specs=[vmem] * 12,
        scratch_shapes=[
            pltpu.VMEM((heads, 2, width, width), HALF),
            pltpu.VMEM((heads, 2, width, width), HALF),
            pltpu.VMEM((heads, 2, width, width), HALF),
            pltpu.SemaphoreType.DMA((heads, 4)),
            pltpu.SemaphoreType.DMA((heads,)),
            pltpu.SemaphoreType.DMA((heads,)),
            pltpu.SemaphoreType.DMA((heads,)),
            pltpu.SemaphoreType.DMA((heads,)),
        ],
        compiler_params=pltpu.CompilerParams(collective_id=0, has_side_effects=True, vmem_limit_bytes=12 * 2**20),
        name="states",
    )(queries, key_rows, value_rows, out_grad)
    block = pl.BlockSpec((1, length, width), lambda h: (h, 0, 0))
    return pl.pallas_call(
        finish_kernel,
        grid=(heads,),
        out_shape=[jax.ShapeDtypeStruct((heads, length, width), HALF)] * 4,
        in_specs=[vmem] * 12,
        out_specs=[block] * 4,
        compiler_params=pltpu.CompilerParams(vmem_limit_bytes=12 * 2**20),
        name="finish",
    )(*held)


def solution(mesh):
    side = 4
    placed = P(None, ("dp", "seq"), None)
    return jax.shard_map(
        functools.partial(on_device, side),
        mesh=mesh,
        in_specs=(placed,) * 4,
        out_specs=(placed,) * 4,
        check_vma=False,
    )
```

time: 250 us -> 52 us (0.21)
  waiting for transfers between devices: 130 us -> 0 us
  matrix products: 91.8 us -> 0 us
  Pallas kernels: 0 us -> 50.8 us
  between operations: 14.1 us -> 0.64 us
  other arithmetic: 10.7 us -> 0 us
    all_gather x2 -> x0, waiting for transfers between devices: 130 us -> none  [the longest x1 66.5 us: on_device(): all_keys = lax.all_gather(key_state[None], 'seq', axis=0, tiled=True)]
    dot_general x44 -> x0, matrix products: 91.8 us -> none  [the longest x4 10.5 us: group_terms(): jnp.einsum('hts,htd->hsd', masked, g_blk, preferred_element_type=wide)]
    pallas_call x0 -> x2, Pallas kernels: none -> 50.8 us  [the longest x1 41 us: on_device(): pl.pallas_call(functools.partial(states_kernel, side), out_shape=rows + p...]
    convert_element_type x4 -> x0, other arithmetic: 9.95 us -> none  [the longest x1 5.25 us: on_device(): (scale[None, :, None] * inner.reshape(heads, length, width)).astype(jnp.b...]
  transfers between devices with their start and end apart: 2 -> 0, of which waited for: 2 -> 0; matrix products, arithmetic and copies ran while one was open for 6% -> 0% of each run, Pallas kernels for 0% -> 0%
where the time goes in v1:
time: 52 us; the launch traced here: 51.4 us
  Pallas kernels  50.8 us (98%)
  between operations  0.64 us (1%)
    pallas_call x1, Pallas kernels, on_device(): pl.pallas_call(functools.partial(states_kernel, side), out_shape=rows + p...  41 us
    pallas_call x1, Pallas kernels, on_device(): pl.pallas_call(finish_kernel, grid=(heads,), out_shape=[jax.ShapeDtypeStr...  9.83 us

profile of v1, /device:TPU:0, one launch (start us, length us, event | category | flops | bytes accessed | tf_op | source)
XLA Modules:
  0.0 51.4 jit_solution(8972982282995549345)
XLA Ops:
  0.6 41.0 %states.1 = (bf16[16,768,128]{2,1,0:T(8,128)(2,1)S(1)}, bf16[16,768,128]{2,1,0:T(8,128)(2,1)S(1)}, bf16[16,768,128]{2,1,0:T(8,128)(2,1)S(1)}, bf16[16,768,128]{2...) custom-call(bf16[16,768,128]{2,1,0:T(8,128)(2,1)} %q_in.1, ...), custom_call_target="tpu_custom_call" | custom-call | tf_op jit(solution)/shard_map/states/pallas_call | solution.py:197
  41.6 9.8 %finish.1 = (bf16[16,768,128]{2,1,0:T(8,128)(2,1)}, bf16[16,768,128]{2,1,0:T(8,128)(2,1)}, bf16[16,768,128]{2,1,0:T(8,128)(2,1)}, bf16[16,768,128]{2,1,0:T(8,128)(2,1)}) custom-call(bf16[16,768,128]{2,1,0:T(8,128)(2,1)S(1)} %get-tuple-element.16.q_ref, bf16[16,768,128]{2,1,0:T(8,128)(2,1)S(1)} %get-tuple-element.17.k_ref, ...), custom_call_target="tpu_custom_call" | custom-call | tf_op jit(solution)/shard_map/finish/pallas_call | solution.py:216

commit v2 on v1

v2 whole, which is shorter than its diff:
```python
import functools

import jax
import jax.numpy as jnp
from jax import lax
from jax.experimental import pallas as pl
from jax.experimental.pallas import tpu as pltpu
from jax.sharding import PartitionSpec as P

MESH = pl.DeviceIdType.MESH
WIDE = jnp.float32
HALF = jnp.bfloat16
CHUNK = 256
EARLY, MIDDLE = 3, 7
TOGETHER, SLOTS = 2, 4


def nn(a, b):
    return lax.dot_general(a, b, (((1,), (0,)), ((), ())), preferred_element_type=WIDE)


def nt(a, b):
    return lax.dot_general(a, b, (((1,), (1,)), ((), ())), preferred_element_type=WIDE)


def tn(a, b):
    return lax.dot_general(a, b, (((0,), (0,)), ((), ())), preferred_element_type=WIDE)


def states_kernel(
    side, q_in, k_in, v_in, g_in,
    q_ref, k_ref, v_ref, g_ref, att_ref, dq_ref, dk_ref, dv_ref, pre_ref, suf_ref, got_ref, scale_ref,
    sent, taken, back, in_sem, send_sem, recv_sem,
):
    heads, length, width = q_in.shape
    chunks = length // CHUNK
    me = lax.axis_index("seq")
    row, col = me // side, me % side
    count = heads
    others = [(dy, dz) for dy in range(side) for dz in range(side) if dy or dz]

    def base(dy):
        return ((row + dy) % side) * side

    def peer(dy, dz):
        return base(dy) + (col + dz) % side

    def loads(dy, kind):
        pairs = (((k_in, k_ref), (v_in, v_ref)), ((q_in, q_ref), (g_in, g_ref)))[kind]
        group = pl.ds(base(dy), side)
        return [
            pltpu.make_async_copy(src.at[group], dst.at[group], in_sem.at[kind, i, dy])
            for i, (src, dst) in enumerate(pairs)
        ]

    def gather(kind, h):
        return pltpu.make_async_remote_copy(
            src_ref=sent.at[kind, h], dst_ref=taken.at[kind, me],
            send_sem=send_sem.at[0, kind], recv_sem=recv_sem.at[0, kind],
            device_id={"seq": h}, device_id_type=MESH,
        )

    def scatter(kind, j):
        return pltpu.make_async_remote_copy(
            src_ref=back.at[kind, j], dst_ref=got_ref.at[kind, me],
            send_sem=send_sem.at[1, kind], recv_sem=recv_sem.at[1, kind],
            device_id={"seq": j}, device_id_type=MESH,
        )

    def all_of(stage, kind):
        many = pl.ds(0, count - 1)
        return pltpu.make_async_remote_copy(
            src_ref=(sent, back)[stage].at[kind, many], dst_ref=(taken, got_ref)[stage].at[kind, many],
            send_sem=send_sem.at[stage, kind], recv_sem=recv_sem.at[stage, kind],
            device_id={"seq": peer(0, 1)}, device_id_type=MESH,
        )

    order = [*range(1, side), 0]
    for dy in order:
        for copy in loads(dy, 0):
            copy.start()

    barrier = pltpu.get_barrier_semaphore()
    for dy, dz in others:
        pl.semaphore_signal(barrier, inc=1, device_id={"seq": peer(dy, dz)}, device_id_type=MESH)

    for dy in order:
        for copy in loads(dy, 1):
            copy.start()

    position = (me * length + lax.broadcasted_iota(jnp.int32, (length, width), 0)).astype(WIDE)
    scale_ref[...] = 1.0 / jnp.sqrt(width * (position + 1.0))

    def key_state(h):
        total = None
        for c in range(chunks):
            rows = pl.ds(c * CHUNK, CHUNK)
            if c:
                pre_ref[h, c - 1] = total
            part = tn(k_ref[h, rows, :], v_ref[h, rows, :])
            total = part if total is None else total + part
        sent[0, h] = total.astype(HALF)

    def grad_state(h):
        total = None
        for c in reversed(range(chunks)):
            rows = pl.ds(c * CHUNK, CHUNK)
            scaled = (scale_ref[rows, :] * g_ref[h, rows, :].astype(WIDE)).astype(HALF)
            g_ref[h, rows, :] = scaled
            if c < chunks - 1:
                suf_ref[h, c] = total
            part = tn(q_ref[h, rows, :], scaled)
            total = part if total is None else total + part
        sent[1, h] = total.astype(HALF)

    for kind in range(2):

        @pl.loop(0, side)
        def _(t):
            dy = (t + 1) % side
            for copy in loads(dy, kind):
                copy.wait()

            @pl.when(t > 0)
            def _():
                if kind == 0:

                    @pl.when(t == 1)
                    def _():
                        pl.semaphore_wait(barrier, count - 1)

                for dz in range(side):
                    gather(kind, peer(t, dz)).start()

            for dz in range(side):
                (key_state, grad_state)[kind](peer(dy, dz))

        taken[kind, me] = sent[kind, me]
        for dz in range(1, side):
            gather(kind, peer(0, dz)).start()

    causal = lax.broadcasted_iota(jnp.int32, (CHUNK, CHUNK), 0) >= lax.broadcasted_iota(
        jnp.int32, (CHUNK, CHUNK), 1
    )

    def inside(start, stop):
        @pl.loop(start, stop)
        def _(h):
            for c in range(chunks):
                rows = pl.ds(c * CHUNK, CHUNK)
                q, k, v, g = q_ref[h, rows, :], k_ref[h, rows, :], v_ref[h, rows, :], g_ref[h, rows, :]
                scores = jnp.where(causal, nt(q, k), 0.0).astype(HALF)
                dots = jnp.where(causal, nt(g, v), 0.0).astype(HALF)
                att_ref[h, rows, :] = nn(scores, v)
                dq_ref[h, rows, :] = nn(dots, k)
                dk_ref[h, rows, :] = tn(dots, q)
                dv_ref[h, rows, :] = tn(scores, g)

    def give_back(kind):
        all_of(0, kind).wait_recv()
        total = jnp.zeros((width, width), WIDE)
        for j in range(count) if kind == 0 else reversed(range(count)):
            back[kind, j] = total.astype(HALF)
            total = total + taken[kind, j].astype(WIDE)
        for dy, dz in others:
            scatter(kind, peer(dy, dz)).start()
        got_ref[kind, me] = back[kind, me]

    inside(0, EARLY)
    give_back(0)
    inside(EARLY, MIDDLE)
    give_back(1)
    inside(MIDDLE, heads)
    for kind in range(2):
        all_of(1, kind).wait_recv()
        for stage in range(2):
            all_of(stage, kind).wait_send()


def finish_kernel(
    q_ref, k_ref, v_ref, g_ref, att_in, dq_in, dk_in, dv_in, pre_ref, suf_ref, got_ref, scale_ref,
    att_out, dq_out, dk_out, dv_out, att_ref, dq_ref, dk_ref, dv_ref, out_sem,
):
    heads, length, _ = q_ref.shape
    chunks = length // CHUNK

    def stores(h):
        pairs = ((att_ref, att_out), (dq_ref, dq_out), (dk_ref, dk_out), (dv_ref, dv_out))
        return [
            pltpu.make_async_copy(src.at[h % SLOTS], dst.at[h], out_sem.at[i, h % SLOTS])
            for i, (src, dst) in enumerate(pairs)
        ]

    def finish(h):
        slot = h % SLOTS
        prefix, suffix = got_ref[0, h].astype(WIDE), got_ref[1, h].astype(WIDE)
        for c in range(chunks):
            rows = pl.ds(c * CHUNK, CHUNK)
            before = (prefix + pre_ref[h, c - 1] if c else prefix).astype(HALF)
            after = (suffix + suf_ref[h, c] if c < chunks - 1 else suffix).astype(HALF)
            q, k, v, g = q_ref[h, rows, :], k_ref[h, rows, :], v_ref[h, rows, :], g_ref[h, rows, :]
            att_ref[slot, rows, :] = (scale_ref[rows, :] * (att_in[h, rows, :] + nn(q, before))).astype(HALF)
            dq_ref[slot, rows, :] = (dq_in[h, rows, :] + nt(g, before)).astype(HALF)
            dk_ref[slot, rows, :] = (dk_in[h, rows, :] + nt(v, after)).astype(HALF)
            dv_ref[slot, rows, :] = (dv_in[h, rows, :] + nn(k, after)).astype(HALF)

    @pl.loop(0, heads // TOGETHER)
    def _(i):
        @pl.when(i >= SLOTS // TOGETHER)
        def _():
            for b in range(TOGETHER):
                for copy in stores(i * TOGETHER + b - SLOTS):
                    copy.wait()

        for b in range(TOGETHER):
            finish(i * TOGETHER + b)
        for b in range(TOGETHER):
            for copy in stores(i * TOGETHER + b):
                copy.start()

    @pl.loop(heads - SLOTS, heads)
    def _(h):
        for copy in stores(h):
            copy.wait()


def on_device(side, queries, key_rows, value_rows, out_grad):
    heads, length, width = queries.shape
    chunks = length // CHUNK
    rows = [pltpu.VMEM((heads, length, width), HALF)] * 4
    parts = [pltpu.VMEM((heads, length, width), WIDE)] * 4
    inner = [pltpu.VMEM((heads, chunks - 1, width, width), WIDE)] * 2
    got = [pltpu.VMEM((2, heads, width, width), HALF)]
    scale = [pltpu.VMEM((length, width), WIDE)]
    vmem = pl.BlockSpec(memory_space=pltpu.VMEM)
    hbm = pl.BlockSpec(memory_space=pl.ANY)
    held = pl.pallas_call(
        functools.partial(states_kernel, side),
        out_shape=rows + parts + inner + got + scale,
        in_specs=[hbm] * 4,
        out_specs=[vmem] * 12,
        scratch_shapes=[pltpu.VMEM((2, heads, width, width), HALF)] * 3
        + [
            pltpu.SemaphoreType.DMA((2, 2, side)),
            pltpu.SemaphoreType.DMA((2, 2)),
            pltpu.SemaphoreType.DMA((2, 2)),
        ],
        compiler_params=pltpu.CompilerParams(collective_id=0, has_side_effects=True, vmem_limit_bytes=12 * 2**20),
        name="states",
    )(queries, key_rows, value_rows, out_grad)
    return pl.pallas_call(
        finish_kernel,
        out_shape=[jax.ShapeDtypeStruct((heads, length, width), HALF)] * 4,
        in_specs=[vmem] * 12,
        out_specs=[hbm] * 4,
        scratch_shapes=[pltpu.VMEM((SLOTS, length, width), HALF)] * 4 + [pltpu.SemaphoreType.DMA((4, SLOTS))],
        compiler_params=pltpu.CompilerParams(vmem_limit_bytes=12 * 2**20),
        name="finish",
    )(*held)


def solution(mesh):
    side = 4
    placed = P(None, ("dp", "seq"), None)
    return jax.shard_map(
        functools.partial(on_device, side),
        mesh=mesh,
        in_specs=(placed,) * 4,
        out_specs=(placed,) * 4,
        check_vma=False,
    )
```

time: 52 us -> 41.8 us (0.80)
  Pallas kernels: 50.8 us -> 41.1 us
    pallas_call x1, Pallas kernels: 41 us -> 33.8 us  [on_device(): pl.pallas_call(functools.partial(states_kernel, side), out_shape=rows + p...]
    pallas_call x1, Pallas kernels: 9.83 us -> 7.26 us  [on_device(): pl.pallas_call(finish_kernel, out_shape=[jax.ShapeDtypeStruct((heads, len...]
where the time goes in v2:
time: 41.8 us; the launch traced here: 41.7 us
  Pallas kernels  41.1 us (98%)
  between operations  0.64 us (2%)
    pallas_call x1, Pallas kernels, on_device(): pl.pallas_call(functools.partial(states_kernel, side), out_shape=rows + p...  33.8 us
    pallas_call x1, Pallas kernels, on_device(): pl.pallas_call(finish_kernel, out_shape=[jax.ShapeDtypeStruct((heads, len...  7.26 us

profile of v2, /device:TPU:0, one launch (start us, length us, event | category | flops | bytes accessed | tf_op | source)
XLA Modules:
  0.0 41.7 jit_solution(5241649272638847873)
XLA Ops:
  0.6 33.8 %states.1 = (bf16[16,768,128]{2,1,0:T(8,128)(2,1)S(1)}, bf16[16,768,128]{2,1,0:T(8,128)(2,1)S(1)}, bf16[16,768,128]{2,1,0:T(8,128)(2,1)S(1)}, bf16[16,768,128]{2...) custom-call(bf16[16,768,128]{2,1,0:T(8,128)(2,1)} %q_in.1, ...), custom_call_target="tpu_custom_call" | custom-call | tf_op jit(solution)/shard_map/states/pallas_call | solution.py:237
  34.5 7.3 %finish.1 = (bf16[16,768,128]{2,1,0:T(8,128)(2,1)}, bf16[16,768,128]{2,1,0:T(8,128)(2,1)}, bf16[16,768,128]{2,1,0:T(8,128)(2,1)}, bf16[16,768,128]{2,1,0:T(8,128)(2,1)}) custom-call(bf16[16,768,128]{2,1,0:T(8,128)(2,1)S(1)} %get-tuple-element.16.q_ref, bf16[16,768,128]{2,1,0:T(8,128)(2,1)S(1)} %get-tuple-element.17.k_ref, ...), custom_call_target="tpu_custom_call" | custom-call | tf_op jit(solution)/shard_map/finish/pallas_call | solution.py:251

commit v3 on v2

--- a/solution.py
+++ b/solution.py
@@ -11,8 +11,8 @@
 WIDE = jnp.float32
 HALF = jnp.bfloat16
 CHUNK = 256
-EARLY, MIDDLE = 3, 7
-TOGETHER, SLOTS = 2, 4
+EARLY, MIDDLE = 5, 10
+TOGETHER, SLOTS = 2, 16
 
 
 def nn(a, b):
@@ -29,7 +29,8 @@
 
 def states_kernel(
     side, q_in, k_in, v_in, g_in,
-    q_ref, k_ref, v_ref, g_ref, att_ref, dq_ref, dk_ref, dv_ref, pre_ref, suf_ref, got_ref, scale_ref,
+    k_ref, v_ref, att_ref, dq_ref, dk_ref, dv_ref, suf_ref, after_ref,
+    q_ref, g_ref, att_part, dq_part, pre_ref, before_ref, scale_ref,
     sent, taken, back, in_sem, send_sem, recv_sem,
 ):
     heads, length, width = q_in.shape
@@ -37,6 +38,7 @@
     me = lax.axis_index("seq")
     row, col = me // side, me % side
     count = heads
+    got = (before_ref, after_ref)
     others = [(dy, dz) for dy in range(side) for dz in range(side) if dy or dz]
 
     def base(dy):
@@ -62,7 +64,7 @@
 
     def scatter(kind, j):
         return pltpu.make_async_remote_copy(
-            src_ref=back.at[kind, j], dst_ref=got_ref.at[kind, me],
+            src_ref=back.at[kind, j], dst_ref=got[kind].at[me],
             send_sem=send_sem.at[1, kind], recv_sem=recv_sem.at[1, kind],
             device_id={"seq": j}, device_id_type=MESH,
         )
@@ -70,7 +72,8 @@
     def all_of(stage, kind):
         many = pl.ds(0, count - 1)
         return pltpu.make_async_remote_copy(
-            src_ref=(sent, back)[stage].at[kind, many], dst_ref=(taken, got_ref)[stage].at[kind, many],
+            src_ref=(sent, back)[stage].at[kind, many],
+            dst_ref=got[kind].at[many] if stage else taken.at[kind, many],
             send_sem=send_sem.at[stage, kind], recv_sem=recv_sem.at[stage, kind],
             device_id={"seq": peer(0, 1)}, device_id_type=MESH,
         )
@@ -146,15 +149,33 @@
     def inside(start, stop):
         @pl.loop(start, stop)
         def _(h):
+            def load(c):
+                rows = pl.ds(c * CHUNK, CHUNK)
+                return q_ref[h, rows, :], k_ref[h, rows, :], v_ref[h, rows, :], g_ref[h, rows, :]
+
+            def weigh(c):
+                q, k, v, g = load(c)
+                return (
+                    jnp.where(causal, nt(q, k), 0.0).astype(HALF), jnp.where(causal, nt(g, v), 0.0).astype(HALF)
+                )
+
+            def apply(c, scores, dots):
+                rows = pl.ds(c * CHUNK, CHUNK)
+                q, k, v, g = load(c)
+                hf = CHUNK // 2
+                top, low = pl.ds(c * CHUNK, hf), pl.ds(c * CHUNK + hf, hf)
+                att_part[h, top, :] = nn(scores[:hf, :hf], v[:hf])
+                att_part[h, low, :] = nn(scores[hf:], v)
+                dq_part[h, top, :] = nn(dots[:hf, :hf], k[:hf])
+                dq_part[h, low, :] = nn(dots[hf:], k)
+                dk_ref[h, top, :] = tn(dots[:, :hf], q)
+                dk_ref[h, low, :] = tn(dots[hf:, hf:], q[hf:])
+                dv_ref[h, top, :] = tn(scores[:, :hf], g)
+                dv_ref[h, low, :] = tn(scores[hf:, hf:], g[hf:])
+
+            held = [weigh(c) for c in range(chunks)]
             for c in range(chunks):
-                rows = pl.ds(c * CHUNK, CHUNK)
-                q, k, v, g = q_ref[h, rows, :], k_ref[h, rows, :], v_ref[h, rows, :], g_ref[h, rows, :]
-                scores = jnp.where(causal, nt(q, k), 0.0).astype(HALF)
-                dots = jnp.where(causal, nt(g, v), 0.0).astype(HALF)
-                att_ref[h, rows, :] = nn(scores, v)
-                dq_ref[h, rows, :] = nn(dots, k)
-                dk_ref[h, rows, :] = tn(dots, q)
-                dv_ref[h, rows, :] = tn(scores, g)
+                apply(c, *held[c])
 
     def give_back(kind):
         all_of(0, kind).wait_recv()
@@ -164,45 +185,63 @@
             total = total + taken[kind, j].astype(WIDE)
         for dy, dz in others:
             scatter(kind, peer(dy, dz)).start()
-        got_ref[kind, me] = back[kind, me]
+        got[kind][me] = back[kind, me]
+
+    def finish(h):
+        prefix = before_ref[h].astype(WIDE)
+        for c in range(chunks):
+            rows = pl.ds(c * CHUNK, CHUNK)
+            before = (prefix + pre_ref[h, c - 1] if c else prefix).astype(HALF)
+            q, g = q_ref[h, rows, :], g_ref[h, rows, :]
+            att_ref[h, rows, :] = (scale_ref[rows, :] * (att_part[h, rows, :] + nn(q, before))).astype(HALF)
+            dq_ref[h, rows, :] = (dq_part[h, rows, :] + nt(g, before)).astype(HALF)
 
     inside(0, EARLY)
     give_back(0)
     inside(EARLY, MIDDLE)
     give_back(1)
     inside(MIDDLE, heads)
+    all_of(1, 0).wait_recv()
+
+    @pl.loop(0, heads // TOGETHER)
+    def _(i):
+        for b in range(TOGETHER):
+            finish(i * TOGETHER + b)
+
+    all_of(1, 1).wait_recv()
     for kind in range(2):
-        all_of(1, kind).wait_recv()
         for stage in range(2):
             all_of(stage, kind).wait_send()
 
 
 def finish_kernel(
-    q_ref, k_ref, v_ref, g_ref, att_in, dq_in, dk_in, dv_in, pre_ref, suf_ref, got_ref, scale_ref,
-    att_out, dq_out, dk_out, dv_out, att_ref, dq_ref, dk_ref, dv_ref, out_sem,
+    k_ref, v_ref, att_ref, dq_ref, dk_part, dv_part, suf_ref, after_ref,
+    att_out, dq_out, dk_out, dv_out, dk_ref, dv_ref, whole_sem, out_sem,
 ):
-    heads, length, _ = q_ref.shape
+    heads, length, _ = k_ref.shape
     chunks = length // CHUNK
+    wholes = [
+        pltpu.make_async_copy(src, dst, whole_sem.at[i])
+        for i, (src, dst) in enumerate(((att_ref, att_out), (dq_ref, dq_out)))
+    ]
+    for copy in wholes:
+        copy.start()
 
     def stores(h):
-        pairs = ((att_ref, att_out), (dq_ref, dq_out), (dk_ref, dk_out), (dv_ref, dv_out))
         return [
             pltpu.make_async_copy(src.at[h % SLOTS], dst.at[h], out_sem.at[i, h % SLOTS])
-            for i, (src, dst) in enumerate(pairs)
+            for i, (src, dst) in enumerate(((dk_ref, dk_out), (dv_ref, dv_out)))
         ]
 
     def finish(h):
         slot = h % SLOTS
-        prefix, suffix = got_ref[0, h].astype(WIDE), got_ref[1, h].astype(WIDE)
+        suffix = after_ref[h].astype(WIDE)
         for c in range(chunks):
             rows = pl.ds(c * CHUNK, CHUNK)
-            before = (prefix + pre_ref[h, c - 1] if c else prefix).astype(HALF)
             after = (suffix + suf_ref[h, c] if c < chunks - 1 else suffix).astype(HALF)
-            q, k, v, g = q_ref[h, rows, :], k_ref[h, rows, :], v_ref[h, rows, :], g_ref[h, rows, :]
-            att_ref[slot, rows, :] = (scale_ref[rows, :] * (att_in[h, rows, :] + nn(q, before))).astype(HALF)
-            dq_ref[slot, rows, :] = (dq_in[h, rows, :] + nt(g, before)).astype(HALF)
-            dk_ref[slot, rows, :] = (dk_in[h, rows, :] + nt(v, after)).astype(HALF)
-            dv_ref[slot, rows, :] = (dv_in[h, rows, :] + nn(k, after)).astype(HALF)
+            k, v = k_ref[h, rows, :], v_ref[h, rows, :]
+            dk_ref[slot, rows, :] = (dk_part[h, rows, :] + nt(v, after)).astype(HALF)
+            dv_ref[slot, rows, :] = (dv_part[h, rows, :] + nn(k, after)).astype(HALF)
 
     @pl.loop(0, heads // TOGETHER)
     def _(i):
@@ -223,38 +262,44 @@
         for copy in stores(h):
             copy.wait()
 
+    for copy in wholes:
+        copy.wait()
+
 
 def on_device(side, queries, key_rows, value_rows, out_grad):
     heads, length, width = queries.shape
     chunks = length // CHUNK
-    rows = [pltpu.VMEM((heads, length, width), HALF)] * 4
-    parts = [pltpu.VMEM((heads, length, width), WIDE)] * 4
-    inner = [pltpu.VMEM((heads, chunks - 1, width, width), WIDE)] * 2
-    got = [pltpu.VMEM((2, heads, width, width), HALF)]
-    scale = [pltpu.VMEM((length, width), WIDE)]
+    row = pltpu.VMEM((heads, length, width), HALF)
+    part = pltpu.VMEM((heads, length, width), WIDE)
+    inner = pltpu.VMEM((heads, chunks - 1, width, width), WIDE)
+    state = pltpu.VMEM((heads, width, width), HALF)
     vmem = pl.BlockSpec(memory_space=pltpu.VMEM)
     hbm = pl.BlockSpec(memory_space=pl.ANY)
     held = pl.pallas_call(
         functools.partial(states_kernel, side),
-        out_shape=rows + parts + inner + got + scale,
+        out_shape=[row] * 4 + [part] * 2 + [inner, state],
         in_specs=[hbm] * 4,
-        out_specs=[vmem] * 12,
-        scratch_shapes=[pltpu.VMEM((2, heads, width, width), HALF)] * 3
+        out_specs=[vmem] * 8,
+        scratch_shapes=[row] * 2
+        + [part] * 2
+        + [inner, state, pltpu.VMEM((length, width), WIDE)]
+        + [pltpu.VMEM((2, heads, width, width), HALF)] * 3
         + [
             pltpu.SemaphoreType.DMA((2, 2, side)),
             pltpu.SemaphoreType.DMA((2, 2)),
             pltpu.SemaphoreType.DMA((2, 2)),
         ],
-        compiler_params=pltpu.CompilerParams(collective_id=0, has_side_effects=True, vmem_limit_bytes=12 * 2**20),
+        compiler_params=pltpu.CompilerParams(collective_id=0, has_side_effects=True, vmem_limit_bytes=26 * 2**20),
         name="states",
     )(queries, key_rows, value_rows, out_grad)
     return pl.pallas_call(
         finish_kernel,
         out_shape=[jax.ShapeDtypeStruct((heads, length, width), HALF)] * 4,
-        in_specs=[vmem] * 12,
+        in_specs=[vmem] * 8,
         out_specs=[hbm] * 4,
-        scratch_shapes=[pltpu.VMEM((SLOTS, length, width), HALF)] * 4 + [pltpu.SemaphoreType.DMA((4, SLOTS))],
-        compiler_params=pltpu.CompilerParams(vmem_limit_bytes=12 * 2**20),
+        scratch_shapes=[pltpu.VMEM((SLOTS, length, width), HALF)] * 2
+        + [pltpu.SemaphoreType.DMA((2,)), pltpu.SemaphoreType.DMA((2, SLOTS))],
+        compiler_params=pltpu.CompilerParams(vmem_limit_bytes=8 * 2**20),
         name="finish",
     )(*held)
 

time: 41.8 us -> 38.1 us (0.911)
  Pallas kernels: 41.1 us -> 37.4 us
    pallas_call x1, Pallas kernels: 7.26 us -> 4.89 us  [on_device(): pl.pallas_call(finish_kernel, out_shape=[jax.ShapeDtypeStruct((heads, len...]
    pallas_call x1, Pallas kernels: 33.8 us -> 32.5 us  [on_device(): pl.pallas_call(functools.partial(states_kernel, side), out_shape=[row] *...]
where the time goes in v3:
time: 38.1 us; the launch traced here: 38 us
  Pallas kernels  37.4 us (98%)
  between operations  0.64 us (2%)
    pallas_call x1, Pallas kernels, on_device(): pl.pallas_call(functools.partial(states_kernel, side), out_shape=[row] *...  32.5 us
    pallas_call x1, Pallas kernels, on_device(): pl.pallas_call(finish_kernel, out_shape=[jax.ShapeDtypeStruct((heads, len...  4.89 us

profile of v3, /device:TPU:0, one launch (start us, length us, event | category | flops | bytes accessed | tf_op | source)
XLA Modules:
  0.0 38.0 jit_solution(12211286869292521009)
XLA Ops:
  0.6 32.5 %states.1 = (bf16[16,768,128]{2,1,0:T(8,128)(2,1)S(1)}, bf16[16,768,128]{2,1,0:T(8,128)(2,1)S(1)}, bf16[16,768,128]{2,1,0:T(8,128)(2,1)S(1)}, bf16[16,768,128]{2...) custom-call(bf16[16,768,128]{2,1,0:T(8,128)(2,1)} %q_in.1, ...), custom_call_target="tpu_custom_call" | custom-call | tf_op jit(solution)/shard_map/states/pallas_call | solution.py:278
  33.1 4.9 %finish.1 = (bf16[16,768,128]{2,1,0:T(8,128)(2,1)}, bf16[16,768,128]{2,1,0:T(8,128)(2,1)}, bf16[16,768,128]{2,1,0:T(8,128)(2,1)}, bf16[16,768,128]{2,1,0:T(8,128)(2,1)}) custom-call(bf16[16,768,128]{2,1,0:T(8,128)(2,1)S(1)} %get-tuple-element.12.k_ref, bf16[16,768,128]{2,1,0:T(8,128)(2,1)S(1)} %get-tuple-element.13.v_ref, ...), custom_call_target="tpu_custom_call" | custom-call | tf_op jit(solution)/shard_map/finish/pallas_call | solution.py:295

commit v4 on v3

--- a/solution.py
+++ b/solution.py
@@ -69,8 +69,11 @@
             device_id={"seq": j}, device_id_type=MESH,
         )
 
-    def all_of(stage, kind):
-        many = pl.ds(0, count - 1)
+    unused = (count - 1, 0)
+    unneeded = (0, count - 1)
+
+    def all_of(stage, kind, blocks=count - 1):
+        many = pl.ds(0, blocks)
         return pltpu.make_async_remote_copy(
             src_ref=(sent, back)[stage].at[kind, many],
             dst_ref=got[kind].at[many] if stage else taken.at[kind, many],
@@ -132,15 +135,20 @@
                     def _():
                         pl.semaphore_wait(barrier, count - 1)
 
-                for dz in range(side):
-                    gather(kind, peer(t, dz)).start()
+                @pl.when(me != unused[kind])
+                def _():
+                    for dz in range(side):
+                        gather(kind, peer(t, dz)).start()
 
             for dz in range(side):
                 (key_state, grad_state)[kind](peer(dy, dz))
 
         taken[kind, me] = sent[kind, me]
-        for dz in range(1, side):
-            gather(kind, peer(0, dz)).start()
+
+        @pl.when(me != unused[kind])
+        def _():
+            for dz in range(1, side):
+                gather(kind, peer(0, dz)).start()
 
     causal = lax.broadcasted_iota(jnp.int32, (CHUNK, CHUNK), 0) >= lax.broadcasted_iota(
         jnp.int32, (CHUNK, CHUNK), 1
@@ -178,14 +186,30 @@
                 apply(c, *held[c])
 
     def give_back(kind):
-        all_of(0, kind).wait_recv()
+        @pl.when(me == unused[kind])
+        def _():
+            all_of(0, kind).wait_recv()
+
+        @pl.when(me != unused[kind])
+        def _():
+            all_of(0, kind, count - 2).wait_recv()
+
         total = jnp.zeros((width, width), WIDE)
         for j in range(count) if kind == 0 else reversed(range(count)):
             back[kind, j] = total.astype(HALF)
-            total = total + taken[kind, j].astype(WIDE)
+            if j != unused[kind]:
+                total = total + taken[kind, j].astype(WIDE)
         for dy, dz in others:
-            scatter(kind, peer(dy, dz)).start()
+
+            @pl.when(peer(dy, dz) != unneeded[kind])
+            def _():
+                scatter(kind, peer(dy, dz)).start()
+
         got[kind][me] = back[kind, me]
+
+        @pl.when(me == unneeded[kind])
+        def _():
+            got[kind][...] = jnp.zeros((heads, width, width), HALF)
 
     def finish(h):
         prefix = before_ref[h].astype(WIDE)
@@ -196,22 +220,37 @@
             att_ref[h, rows, :] = (scale_ref[rows, :] * (att_part[h, rows, :] + nn(q, before))).astype(HALF)
             dq_ref[h, rows, :] = (dq_part[h, rows, :] + nt(g, before)).astype(HALF)
 
+    def take(kind):
+        @pl.when(me != unneeded[kind])
+        def _():
+            all_of(1, kind).wait_recv()
+
     inside(0, EARLY)
     give_back(0)
     inside(EARLY, MIDDLE)
     give_back(1)
     inside(MIDDLE, heads)
-    all_of(1, 0).wait_recv()
+    take(0)
 
     @pl.loop(0, heads // TOGETHER)
     def _(i):
         for b in range(TOGETHER):
             finish(i * TOGETHER + b)
 
-    all_of(1, 1).wait_recv()
+    take(1)
     for kind in range(2):
-        for stage in range(2):
-            all_of(stage, kind).wait_send()
+
+        @pl.when(me != unused[kind])
+        def _():
+            all_of(0, kind).wait_send()
+
+        @pl.when(me == unneeded[kind])
+        def _():
+            all_of(1, kind).wait_send()
+
+        @pl.when(me != unneeded[kind])
+        def _():
+            all_of(1, kind, count - 2).wait_send()
 
 
 def finish_kernel(

time: 38.1 us -> 38.2 us (level)
  the two profiles are of different devices: /device:TPU:0 before, /device:TPU:30 now
where the time goes in v4:
time: 38.2 us; the launch traced here: 38.1 us
  Pallas kernels  37.5 us (98%)
  between operations  0.64 us (2%)
    pallas_call x1, Pallas kernels, on_device(): pl.pallas_call(functools.partial(states_kernel, side), out_shape=[row] *...  32.6 us
    pallas_call x1, Pallas kernels, on_device(): pl.pallas_call(finish_kernel, out_shape=[jax.ShapeDtypeStruct((heads, len...  4.89 us

profile of v4, /device:TPU:30, one launch (start us, length us, event | category | flops | bytes accessed | tf_op | source)
XLA Modules:
  0.0 38.1 jit_solution(6443494492235971666)
XLA Ops:
  0.6 32.6 %states.1 = (bf16[16,768,128]{2,1,0:T(8,128)(2,1)S(1)}, bf16[16,768,128]{2,1,0:T(8,128)(2,1)S(1)}, bf16[16,768,128]{2,1,0:T(8,128)(2,1)S(1)}, bf16[16,768,128]{2...) custom-call(bf16[16,768,128]{2,1,0:T(8,128)(2,1)} %q_in.1, ...), custom_call_target="tpu_custom_call" | custom-call | tf_op jit(solution)/shard_map/states/pallas_call | solution.py:317
  33.2 4.9 %finish.1 = (bf16[16,768,128]{2,1,0:T(8,128)(2,1)}, bf16[16,768,128]{2,1,0:T(8,128)(2,1)}, bf16[16,768,128]{2,1,0:T(8,128)(2,1)}, bf16[16,768,128]{2,1,0:T(8,128)(2,1)}) custom-call(bf16[16,768,128]{2,1,0:T(8,128)(2,1)S(1)} %get-tuple-element.12.k_ref, bf16[16,768,128]{2,1,0:T(8,128)(2,1)S(1)} %get-tuple-element.13.v_ref, ...), custom_call_target="tpu_custom_call" | custom-call | tf_op jit(solution)/shard_map/finish/pallas_call | solution.py:334
